TPU v7x, 32 devices: a whole 2x2x4 slice. The times are simulated.
32 devices in a mesh: leaf: 4 (over x, core), row: 4 (over z), col: 2 (over y).
Axes of the slice: x: 2, y: 2, z: 4, core: 2. Of those that a mesh axis runs over, the one named last changes fastest.
Arguments:
- widths: int32 [15], replicated, may hold values from 1024 to 2048, as said below
- bottom_lists: int32 [8, 32], P('leaf'), may hold values from 0 to 47, as said below
- root_inverse: bfloat16 [2048, 2048], P('row')
- second_panels: bfloat16 [4, 2048, 1024], P('leaf', 'row', 'col'), may hold values from -0.09375 to 0.09375
- second_inverse: bfloat16 [4, 1024, 2048], P('leaf', 'col', 'row')
- third_panels: bfloat16 [4, 2, 2048, 2048], P('leaf', None, 'row', 'col'), may hold values from -0.09375 to 0.09375
- third_inverse: bfloat16 [4, 2048, 2048], P('leaf', 'col', 'row')
- bottom_panels: bfloat16 [8, 4096, 2048], P('leaf', 'row', 'col'), may hold values from -0.09375 to 0.09375
- bottom_inverse: bfloat16 [8, 2048, 2048], P('leaf', 'col', 'row')
Outputs:
- second_off: bfloat16 [4, 2048, 1024], P('leaf', 'row', 'col')
- second_diag: bfloat16 [4, 1024, 2048], P('leaf', 'col', 'row')
- third_off: bfloat16 [4, 2, 2048, 2048], P('leaf', None, 'row', 'col')
- third_diag: bfloat16 [4, 2048, 2048], P('leaf', 'col', 'row')
- bottom_off: bfloat16 [8, 3, 2048, 2048], P('leaf', None, 'row', 'col')
- bottom_diag: bfloat16 [8, 2048, 2048], P('leaf', 'col', 'row')
Inputs may be any that keep to these rules, and one draw needn't show every extreme that they name: `widths`: some supernode has 2048 columns and some 2048/2. `bottom_lists`: row e lists 32 different blocks of 128 rows of its chain (root, then second-level ancestor, then parent, 16 blocks each) in increasing order; block 0 and all blocks of the parent are always listed.
All inputs are finite; a program needn't handle non-finite values.
Results may differ from a plain program's by a relative error of at most 0.015.
Values may be sent and summed in bfloat16 or wider, within the bound.
No kernel may reach another device: no remote copies, remote signals or barrier semaphores. Data moves between devices by JAX's collectives and lax.ppermute only.
A program may use at most 192 MiB of HBM per device.

v0:
```python
import jax
import jax.numpy as jnp
from jax import lax
from jax.sharding import PartitionSpec as P

NODES = 15
BOTTOM = 8


def partner(block, axis, apart):
    count = lax.axis_size(axis)
    route = []
    for low in range(count):
        high = low | 1 << apart
        if high != low and high < count:
            route += [(low, high), (high, low)]
    return lax.ppermute(block, axis, route)


def node_width(widths, node_at):
    return jnp.sum(jnp.where(jnp.arange(widths.shape[0]) == node_at, widths, 0))


def chain_fold(flat_chain, tile_width, ancestors, shard_piece):
    piece_rows = shard_piece.shape[1]
    picked = jnp.concatenate(
        [
            lax.dynamic_slice_in_dim(flat_chain, level_at * tile_width, piece_rows, 1)
            for level_at in range(ancestors)
        ],
        axis=1,
    )
    stacked = shard_piece.reshape(ancestors * piece_rows, shard_piece.shape[2])
    return jnp.dot(picked, stacked, preferred_element_type=jnp.float32)


def local(
    widths,
    bottom_lists,
    root_inverse,
    second_panels,
    second_inverse,
    third_panels,
    third_inverse,
    bottom_panels,
    bottom_inverse,
):
    group_at = lax.axis_index("leaf")
    row_at = lax.axis_index("row")
    col_at = lax.axis_index("col")
    rows_dev = root_inverse.shape[0]
    tile_width = root_inverse.shape[1]
    half_cols = second_panels.shape[2]
    own_cols = third_panels.shape[3]
    half_at = group_at % 2
    parent_one = 1 + group_at // 2
    node_two = 3 + group_at
    row_first = row_at * rows_dev
    row_index = row_first + jnp.arange(rows_dev)
    root_width = node_width(widths, 0)
    root_mask = (row_index < root_width)[:, None] & (jnp.arange(tile_width) < root_width)[None, :]
    root_block = jnp.where(root_mask, root_inverse, 0)
    width_one = node_width(widths, parent_one)
    mask_rows_one = row_index < width_one
    first_col = half_at * (tile_width // 2) + col_at * half_cols
    mask_cols_one = first_col + jnp.arange(half_cols) < width_one
    panel_one = jnp.where(mask_cols_one[None, :], second_panels[0], 0)
    shard_piece = lax.all_gather(panel_one, "row", axis=0, tiled=True)
    flat_piece = shard_piece
    product_one = jnp.dot(root_block, flat_piece, preferred_element_type=jnp.float32)
    off_one = (-product_one).astype(jnp.bfloat16)
    mine_half = lax.all_gather(off_one, "col", axis=1, tiled=True)
    other_half = partner(mine_half, "leaf", 0)
    off_full = jnp.where(
        half_at == 0,
        jnp.concatenate([mine_half, other_half], 1),
        jnp.concatenate([other_half, mine_half], 1),
    )
    term_one = lax.dot_general(
        panel_one, off_full, (((0,), (0,)), ((), ())), preferred_element_type=jnp.float32
    )
    summed_one = lax.psum_scatter(
        term_one.astype(jnp.bfloat16), "row", scatter_dimension=1, tiled=True
    ).astype(jnp.float32)
    inverse_one = jnp.where(
        mask_cols_one[:, None] & mask_rows_one[None, :], second_inverse[0], 0
    ).astype(jnp.float32)
    diag_one = (inverse_one - summed_one).astype(jnp.bfloat16)
    mine_diag = lax.all_gather(diag_one.T, "col", axis=1, tiled=True)
    other_diag = partner(mine_diag, "leaf", 0)
    diag_full = jnp.where(
        half_at == 0,
        jnp.concatenate([mine_diag, other_diag], 1),
        jnp.concatenate([other_diag, mine_diag], 1),
    )
    second_off = off_one[None]
    second_diag = diag_one[None]
    turned_one = lax.all_to_all(off_full, "row", split_axis=1, concat_axis=0, tiled=True)
    chain_two = jnp.stack(
        [jnp.concatenate([root_block, off_full], 1), jnp.concatenate([turned_one.T, diag_full], 1)],
        0,
    )
    flat_two = chain_two.reshape(2 * rows_dev, 2 * tile_width)
    first_own = col_at * own_cols
    width_two = node_width(widths, node_two)
    mask_cols_two = first_own + jnp.arange(own_cols) < width_two
    panel_two = jnp.where(mask_cols_two[None, None, :], third_panels[0], 0)
    product_two = chain_fold(
        flat_two, tile_width, 2, lax.all_gather(panel_two, "row", axis=1, tiled=True)
    )
    off_two = (-product_two).astype(jnp.bfloat16).reshape(2, rows_dev, own_cols)
    full_two = lax.all_gather(off_two, "col", axis=2, tiled=True)
    term_two = jnp.einsum("kin,kim->nm", panel_two, full_two, preferred_element_type=jnp.float32)
    summed_two = lax.psum_scatter(
        term_two.astype(jnp.bfloat16), "row", scatter_dimension=1, tiled=True
    ).astype(jnp.float32)
    mask_rows_two = row_index < width_two
    inverse_two = jnp.where(
        mask_cols_two[:, None] & mask_rows_two[None, :], third_inverse[0], 0
    ).astype(jnp.float32)
    diag_two = (inverse_two - summed_two).astype(jnp.bfloat16)
    diag_rows_two = lax.all_gather(diag_two.T, "col", axis=1, tiled=True)
    turned_two = lax.all_to_all(full_two, "row", split_axis=2, concat_axis=1, tiled=True)
    lower_two = jnp.transpose(turned_two, (2, 0, 1)).reshape(rows_dev, 2 * tile_width)
    chain_three = jnp.stack(
        [
            jnp.concatenate([chain_two[0], full_two[0]], 1),
            jnp.concatenate([chain_two[1], full_two[1]], 1),
            jnp.concatenate([lower_two, diag_rows_two], 1),
        ],
        0,
    )
    flat_three = chain_three.reshape(3 * rows_dev, 3 * tile_width)
    bottom_dev = bottom_panels.shape[0]
    list_len = bottom_lists.shape[1]
    block_rows = 2 * tile_width // list_len
    node_three = NODES - BOTTOM + bottom_dev * group_at + jnp.arange(bottom_dev)
    width_three = jnp.sum(
        jnp.where(jnp.arange(widths.shape[0])[None, :] == node_three[:, None], widths[None, :], 0),
        1,
    )
    mask_cols_three = (first_own + jnp.arange(own_cols))[None, :] < width_three[:, None]
    panel_three = jnp.where(mask_cols_three[:, None, :], bottom_panels, 0)
    positions = (
        jnp.repeat(bottom_lists, block_rows, axis=1) * block_rows
        + jnp.arange(list_len * block_rows) % block_rows
    )
    own_chain = (jnp.arange(3)[:, None] * tile_width + row_index[None, :]).reshape(-1)
    matches = bottom_lists[:, :, None] == (own_chain // block_rows)[None, None, :]
    member = jnp.any(matches, axis=1)
    slot_index = (
        jnp.sum(jnp.where(matches, jnp.arange(list_len)[None, :, None], 0), axis=1) * block_rows
        + own_chain % block_rows
    )
    shard_piece = lax.all_gather(panel_three, "row", axis=1, tiled=True)
    kept_rows = jnp.zeros((bottom_dev, 3 * rows_dev, own_cols), jnp.bfloat16)
    piece_rows = shard_piece.shape[1]
    columns = jnp.take(flat_three, positions.reshape(-1), axis=1).reshape(
        3 * rows_dev, bottom_dev, piece_rows
    )
    running = jnp.einsum("aec,ecn->ean", columns, shard_piece, preferred_element_type=jnp.float32)
    inside = member & (slot_index >= 0) & (slot_index < piece_rows)
    fetched = jax.vmap(lambda rows_in, picks: jnp.take(rows_in, picks, axis=0))(
        shard_piece, jnp.clip(slot_index, 0, piece_rows - 1)
    )
    kept_rows = jnp.where(inside[:, :, None], fetched, kept_rows)
    product_three, kept_rows = (running, kept_rows)
    chain_rows = kept_rows.reshape(bottom_dev, 3, rows_dev, own_cols)
    off_three = jnp.where(member[:, :, None], -product_three, 0.0).astype(jnp.bfloat16)
    off_three = off_three.reshape(bottom_dev, 3, rows_dev, own_cols)
    full_three = lax.all_gather(off_three, "col", axis=3, tiled=True)
    term_three = jnp.einsum(
        "ekin,ekim->enm", chain_rows, full_three, preferred_element_type=jnp.float32
    )
    summed_three = lax.psum_scatter(
        term_three.astype(jnp.bfloat16), "row", scatter_dimension=2, tiled=True
    ).astype(jnp.float32)
    mask_rows_three = row_index[None, :] < width_three[:, None]
    inverse_three = jnp.where(
        mask_cols_three[:, :, None] & mask_rows_three[:, None, :], bottom_inverse, 0
    ).astype(jnp.float32)
    diag_three = (inverse_three - summed_three).astype(jnp.bfloat16)
    return (second_off, second_diag, off_two[None], diag_two[None], off_three, diag_three)


def solution(mesh):
    in_specs = (
        P(),
        P("leaf", None),
        P("row", None),
        P("leaf", "row", "col"),
        P("leaf", "col", "row"),
        P("leaf", None, "row", "col"),
        P("leaf", "col", "row"),
        P("leaf", "row", "col"),
        P("leaf", "col", "row"),
    )
    out_specs = (
        P("leaf", "row", "col"),
        P("leaf", "col", "row"),
        P("leaf", None, "row", "col"),
        P("leaf", "col", "row"),
        P("leaf", None, "row", "col"),
        P("leaf", "col", "row"),
    )
    return jax.shard_map(local, mesh=mesh, in_specs=in_specs, out_specs=out_specs, check_vma=False)
```

profile of v0, /device:TPU:0, one launch (start us, length us, event | category | flops | bytes accessed | tf_op | source)
XLA Modules:
  0.0 1239.9 jit_solution(15678151634752697169)
XLA Ops:
  15.1 44.9 %all-gather.9.cloned.1.call-done = bf16[2048,512]{0,1:T(8,128)(2,1)} async-done(((bf16[512,512]{0,1:T(8,128)(2,1)}), bf16[2048,512]{0,1:T(8,128)(2,1)}) %all-gather.9.cloned.1.call-update) | async-done | bytes 2097168 | tf_op jit(solution)/shard_map/all_gather | solution.py:68
  63.7 20.2 %all-gather.11.cloned.1.call-done = bf16[512,1024]{1,0:T(8,128)(2,1)} async-done(((bf16[512,512]{1,0:T(8,128)(2,1)}), bf16[512,1024]{1,0:T(8,128)(2,1)}) %all-gather.11.cloned.1.call-update) | async-done | bytes 1048592 | tf_op jit(solution)/shard_map/all_gather | solution.py:72
  96.3 41.0 %reduce-scatter.4.cloned.1.call-done = bf16[512,512]{0,1:T(8,128)(2,1)} async-done(((bf16[512,2048]{0,1:T(8,128)(2,1)}), bf16[512,512]{0,1:T(8,128)(2,1)}) %reduce-scatter.4.cloned.1.call-update) | async-done | bytes 524304 | tf_op jit(solution)/shard_map/reduce_scatter | solution.py:82
  146.5 4.4 all-to-all-start
  151.0 9.4 all-gather.13.cloned.1.call-done
  164.4 75.8 %all-to-all-done = bf16[512,4,512]{2,0,1:T(8,128)(2,1)} async-done(((bf16[512,4,512]{2,0,1:T(8,128)(2,1)}), bf16[512,4,512]{2,0,1:T(8,128)(2,1)}, u32[]{:S(2)}, u32[]{:S(2)}) %all-to-all-start) | async-done | bytes 2097184 | tf_op jit(solution)/shard_map/all_to_all | solution.py:98
  250.5 7.5 pad_maximum_fusion.1
  258.0 76.6 %all-gather.15.cloned.1.call-done = bf16[2,2048,1024]{2,1,0:T(8,128)(2,1)} async-done(((bf16[2,512,1024]{2,1,0:T(8,128)(2,1)}), bf16[2,2048,1024]{2,1,0:T(8,128)(2,1)}) %all-gather.15.cloned.1.call-update) | async-done | bytes 8388624 | tf_op jit(solution)/shard_map/all_gather | solution.py:109
  334.5 14.6 %negate_convert_fusion = bf16[1024,1024]{1,0:T(8,128)(2,1)} fusion(bf16[1024,4096]{1,0:T(8,128)(2,1)} %bitcast.115, bf16[4096,1024]{1,0:T(8,128)(2,1)} %bitcast.128), kind=kOutput, calls=%fused_computation.21 | convolution fusion | flops 8592031744 | bytes 18874368 | tf_op jit(solution)/shard_map/dot_general | solution.py:34
  349.2 12.2 reduce-scatter.6.cloned.1.call-start
  361.4 43.7 %all-gather.17.cloned.1.call-done = bf16[2,512,2048]{2,1,0:T(8,128)(2,1)} async-done(((bf16[2,512,1024]{2,1,0:T(8,128)(2,1)}), bf16[2,512,2048]{2,1,0:T(8,128)(2,1)}) %all-gather.17.cloned.1.call-update) | async-done | bytes 4194320 | tf_op jit(solution)/shard_map/all_gather | solution.py:112
  405.1 9.4 bitcast_convert_fusion.1
  416.6 74.8 %reduce-scatter.6.cloned.1.call-done = bf16[1024,512]{0,1:T(8,128)(2,1)} async-done(((bf16[1024,2048]{0,1:T(8,128)(2,1)}), bf16[1024,512]{0,1:T(8,128)(2,1)}) %reduce-scatter.6.cloned.1.call-update) | async-done | bytes 1048592 | tf_op jit(solution)/shard_map/reduce_scatter | solution.py:114
  496.0 4.4 broadcast_select_fusion
  500.5 11.2 copy.70
  511.8 5.0 all-to-all-start.1
  523.1 5.1 maximum_bitcast_fusion
  528.2 191.2 %all-to-all-done.1 = bf16[2,512,2048]{1,0,2:T(2,128)(2,1)} async-done(((bf16[2,512,2048]{1,0,2:T(2,128)(2,1)}), bf16[2,512,2048]{1,0,2:T(2,128)(2,1)}, u32[]{:S(2)}, u32[]{:S(2)}) %all-to-all-start.1) | async-done | bytes 4194336 | tf_op jit(solution)/shard_map/all_to_all | solution.py:123
  719.4 5.1 copy.85
  724.5 4.5 copy.87
  728.9 6.4 maximum_bitcast_fusion.2
  735.4 12.1 pad_maximum_fusion
  747.5 24.7 %copy.72 = bf16[1536,6144]{0,1:T(8,128)(2,1)} copy(bf16[1536,6144]{1,0:T(8,128)(2,1)} %bitcast.107) | data formatting | bytes 37748736 | tf_op jit(solution)/shard_map/reshape | solution.py:133
  772.2 58.3 %gather_fusion = bf16[8192,1536]{1,0:T(8,128)(2,1)} fusion(bf16[1536,6144]{0,1:T(8,128)(2,1)} %copy.72, s32[8192]{0:T(1024)S(1)} %broadcast_clamp_fusion), kind=kCustom, calls=%fused_computation | custom fusion | bytes 50364416 | tf_op jit(solution)/shard_map/jit(_take)/gather | solution.py:158
  830.5 32.1 %copy.73 = bf16[1536,2,4096]{2,0,1:T(8,128)(2,1)} copy(bf16[1536,2,4096]{0,2,1:T(8,128)(2,1)} %bitcast.106) | data formatting | bytes 50331648 | tf_op jit(solution)/shard_map/jit(_take)/gather | solution.py:158
  862.5 18.1 %all-gather.21.cloned.1.call-done = bf16[2,4096,1024]{2,1,0:T(8,128)(2,1)} async-done(((bf16[2,1024,1024]{2,1,0:T(8,128)(2,1)}), bf16[2,4096,1024]{2,1,0:T(8,128)(2,1)}) %all-gather.21.cloned.1.call-update) | async-done | bytes 16777232 | tf_op jit(solution)/shard_map/all_gather | solution.py:155
  880.7 33.0 %select_convert_fusion = bf16[2,1536,1024]{2,1,0:T(8,128)(2,1)} fusion(bf16[2,4096,1024]{2,1,0:T(8,128)(2,1)} %all-gather.21.cloned.1.call-done, bf16[1536,2,4096]{2,0,1:T(8,128)(2,1)} %copy.73, pred[2,4096]{1,0:T(4,128)(4,1)S(1)} %compare_and_fusion, pred[2,1536]{1,0:T(4,128)(4,1)S(1)} %compare_reduce_fusion), kind=kOutput, calls=%fused_computation.7 | convolution fusion | flops 25791823872 | bytes 48245760 | tf_op jit(solution)/shard_map/aec,ecn->ean/dot_general | solution.py:161
  914.7 62.6 %gather_fusion.1 = bf16[3072,1024]{1,0:T(8,128)(2,1)} fusion(bf16[2,4096,1024]{2,1,0:T(8,128)(2,1)} %all-gather.21.cloned.1.call-done, s32[3072]{0:T(1024)S(1)} %reshape.373), kind=kCustom, calls=%fused_computation.1 | custom fusion | bytes 12607488 | tf_op jit(solution)/shard_map/vmap(jit(_take))/gather | solution.py:163
  977.3 8.7 copy.74
  986.0 79.0 %all-gather.23.cloned.1.call-done = bf16[2,3,512,2048]{3,2,1,0:T(8,128)(2,1)} async-done(((bf16[2,3,512,1024]{3,2,1,0:T(8,128)(2,1)}), bf16[2,3,512,2048]{3,2,1,0:T(8,128)(2,1)}) %all-gather.23.cloned.1.call-update) | async-done | bytes 12582928 | tf_op jit(solution)/shard_map/all_gather | solution.py:171
  1064.9 20.0 %bitcast_convert_fusion = bf16[2,1024,2048]{2,1,0:T(8,128)(2,1)} fusion(bf16[2,3,512,2048]{3,2,1,0:T(8,128)(2,1)} %all-gather.23.cloned.1.call-done, bf16[2,3,512,1024]{2,3,1,0:T(8,128)(2,1)} %copy.74, pred[2,3,512]{2,1,0:T(4,128)(4,1)S(1)} %get-tuple-element.40, pred[2,3,512]{2,1,0:T(4,128)(4,1)S(1)} %get-tuple-element.39), kind=kOutput, calls=%fused_computation.6 | convolution fusion | flops 12895387648 | bytes 27269120 | tf_op jit(solution)/shard_map/ekin,ekim->enm/dot_general | solution.py:172
  1089.2 140.5 %reduce-scatter.8.cloned.1.call-done = bf16[2,1024,512]{2,1,0:T(8,128)(2,1)} async-done(((bf16[2,1024,2048]{2,1,0:T(8,128)(2,1)}), bf16[2,1024,512]{2,1,0:T(8,128)(2,1)}) %reduce-scatter.8.cloned.1.call-update) | async-done | bytes 2097168 | tf_op jit(solution)/shard_map/reduce_scatter | solution.py:175
  (137 shorter events, 68.8 us)
Async XLA Ops:
  7.2 52.8 %all-gather.9.cloned.1.call-start = ((), (), s32[]{:S(2)}) async-start(), calls=%async_computation.5 | async-start | bytes 2621440 | tf_op jit(solution)/shard_map/all_gather | solution.py:68
  11.4 72.5 %all-gather.11.cloned.1.call-start = ((), (), s32[]{:S(2)}) async-start(), calls=%async_computation.6 | async-start | bytes 1572864 | tf_op jit(solution)/shard_map/all_gather | solution.py:72
  63.7 73.6 %reduce-scatter.4.cloned.1.call-start = ((), (), s32[]{:S(2)}) async-start(), calls=%async_computation.7 | async-start | bytes 2621440 | tf_op jit(solution)/shard_map/reduce_scatter | solution.py:82
  83.9 2.9 collective-permute-start
  83.9 6.9 copy-start.10
  86.8 6.7 copy-start.8
  89.5 1.4 copy-start
  93.5 66.9 %all-gather.13.cloned.1.call-start = ((), (), s32[]{:S(2)}) async-start(), calls=%async_computation.8 | async-start | bytes 1572864 | tf_op jit(solution)/shard_map/all_gather | solution.py:89
  96.3 47.2 %copy-start.7 = (bf16[512,1024]{1,0:T(8,128)(2,1)S(1)}, bf16[512,1024]{1,0:T(8,128)(2,1)}, u32[]{:S(2)}) copy-start(bf16[512,1024]{1,0:T(8,128)(2,1)} %all-gather.11.cloned.1.call-done) | copy-start | bytes 3145732
  139.8 194.7 %all-gather.15.cloned.1.call-start = ((), (), s32[]{:S(2)}) async-start(), calls=%async_computation.9 | async-start | bytes 10485760 | tf_op jit(solution)/shard_map/all_gather | solution.py:109
  146.5 93.6 %all-to-all-start = ((bf16[512,4,512]{2,0,1:T(8,128)(2,1)}), bf16[512,4,512]{2,0,1:T(8,128)(2,1)}, u32[]{:S(2)}, u32[]{:S(2)}) async-start(bf16[512,4,512]{2,0,1:T(8,128)(2,1)} %maximum_select_fusion.1), calls=%async_computation.1 | async-start | bytes 4194304 | tf_op jit(solution)/shard_map/all_to_all | solution.py:98
  151.0 254.1 %all-gather.17.cloned.1.call-start = ((), (), s32[]{:S(2)}) async-start(), calls=%async_computation.10 | async-start | bytes 6291456 | tf_op jit(solution)/shard_map/all_gather | solution.py:112
  160.4 83.6 %collective-permute-start.1 = (bf16[512,1024]{1,0:T(8,128)(2,1)}, bf16[512,1024]{1,0:T(8,128)(2,1)}, u32[]{:S(2)}, u32[]{:S(2)}) collective-permute-start(bf16[512,1024]{1,0:T(8,128)(2,1)} %all-gather.13.cloned.1.call-done), channel_id=1, source_target_pairs={{0,8},{8,0},{16,24},{24,16},{1,9},{9,1},{17,25},{25,17},{2,10},{10... | collective-permute-start | bytes 3145736 | tf_op jit(solution)/shard_map/ppermute | solution.py:17
  164.4 79.7 %copy-start.11 = (bf16[512,1024]{1,0:T(8,128)(2,1)S(1)}, bf16[512,1024]{1,0:T(8,128)(2,1)}, u32[]{:S(2)}) copy-start(bf16[512,1024]{1,0:T(8,128)(2,1)} %all-gather.13.cloned.1.call-done) | copy-start | bytes 3145732
  244.0 3.9 copy-start.2
  246.6 1.4 copy-start.4
  349.2 142.3 %reduce-scatter.6.cloned.1.call-start = ((), (), s32[]{:S(2)}) async-start(), calls=%async_computation.11 | async-start | bytes 5242880 | tf_op jit(solution)/shard_map/reduce_scatter | solution.py:114
  414.5 80.1 %copy-start.24 = (s32[15]{0:T(128)S(1)}, s32[15]{0:T(128)}, u32[]{:S(2)}) copy-start(s32[15]{0:T(128)} %param.9) | copy-start | bytes 184
  414.5 314.4 %all-gather.19.cloned.1.call-start = ((), (), s32[]{:S(2)}) async-start(), calls=%async_computation.12 | async-start | bytes 3145728 | tf_op jit(solution)/shard_map/all_gather | solution.py:122
  494.6 386.1 %all-gather.21.cloned.1.call-start = ((), (), s32[]{:S(2)}) async-start(), calls=%async_computation.13 | async-start | bytes 20971520 | tf_op jit(solution)/shard_map/all_gather | solution.py:155
  511.8 6.4 copy-start.20
  511.8 207.6 %all-to-all-start.1 = ((bf16[2,512,2048]{1,0,2:T(2,128)(2,1)}), bf16[2,512,2048]{1,0,2:T(2,128)(2,1)}, u32[]{:S(2)}, u32[]{:S(2)}) async-start(bf16[2,512,2048]{1,0,2:T(2,128)(2,1)} %copy.70), calls=%async_computation.3 | async-start | bytes 8388608 | tf_op jit(solution)/shard_map/all_to_all | solution.py:123
  516.8 548.2 %all-gather.23.cloned.1.call-start = ((), (), s32[]{:S(2)}) async-start(), calls=%async_computation.14 | async-start | bytes 18874368 | tf_op jit(solution)/shard_map/all_gather | solution.py:171
  519.0 2.9 copy-start.1
  519.0 3.5 copy-start.3
  519.0 4.1 copy-start.5
  728.9 6.4 slice-start
  728.9 6.4 slice-start.1
  913.7 316.0 %reduce-scatter.8.cloned.1.call-start = ((), (), s32[]{:S(2)}) async-start(), calls=%async_computation.15 | async-start | bytes 10485760 | tf_op jit(solution)/shard_map/reduce_scatter | solution.py:175
  1084.9 3.0 copy-start.6
  1084.9 144.8 %copy-start.9 = (bf16[2,1024,512]{2,1,0:T(8,128)(2,1)S(1)}, bf16[2,1024,512]{2,1,0:T(8,128)(2,1)}, u32[]{:S(2)}) copy-start(bf16[2,1024,512]{2,1,0:T(8,128)(2,1)} %param.17) | copy-start | bytes 6291460
  1084.9 144.8 %copy-start.15 = (pred[2,1024]{1,0:T(4,128)(4,1)S(1)}, pred[2,1024]{1,0:T(4,128)(4,1)}, u32[]{:S(2)}) copy-start(pred[2,1024]{1,0:T(4,128)(4,1)} %copy-done.14) | copy-start | bytes 6148
  (10 other events, 6.9 us)
Sparse Core Ops, SparseCore 0:
  11.6 48.3 all-gather.8
  63.8 20.0 all-gather.10
  93.6 43.6 reduce-scatter.3
  139.9 20.4 all-gather.12
  161.9 172.6 all-gather.14
  349.3 55.7 all-gather.16
  414.6 76.7 reduce-scatter.5
  494.7 33.6 all-gather.18
  529.9 350.6 all-gather.20
  913.8 151.0 all-gather.22
  1085.1 144.6 reduce-scatter.7
where the time goes:
time: 1250 us; the launch traced here: 1240 us
  waiting for transfers between devices  818 us (65%)
  local copies, waits for them, and re-layouts  231 us (18%)
  matrix products  83.3 us (7%)
  other arithmetic  71.1 us (6%)
  starting transfers between devices  22 us (2%)
  between operations  14.7 us (1%)
    all_to_all x1, waiting for transfers between devices, local(): lax.all_to_all(full_two, 'row', split_axis=2, concat_axis=1, tiled=True)  191 us
    reduce_scatter x1, waiting for transfers between devices, local(): lax.psum_scatter(term_three.astype(jnp.bfloat16), 'row', scatter_dimensio...  141 us
    gather x2, local copies, waits for them, and re-layouts, local(): jnp.take(flat_three, positions.reshape(-1), axis=1)  90.3 us
    all_gather x1, waiting for transfers between devices, local(): full_three = lax.all_gather(off_three, 'col', axis=3, tiled=True)  79 us
    all_gather x1, waiting for transfers between devices, local(): lax.all_gather(panel_two, 'row', axis=1, tiled=True)  76.6 us
    all_to_all x1, waiting for transfers between devices, local(): lax.all_to_all(off_full, 'row', split_axis=1, concat_axis=0, tiled=True)  75.8 us
    reduce_scatter x1, waiting for transfers between devices, local(): lax.psum_scatter(term_two.astype(jnp.bfloat16), 'row', scatter_dimension=...  74.8 us
    gather x3, local copies, waits for them, and re-layouts, local(): jnp.take(rows_in, picks, axis=0)  71.3 us
  transfers between devices with their start and end apart: 15, of which 13 were waited for; matrix products, arithmetic and copies ran while one was open for 23% of the time, Pallas kernels for 0%

commit v1 on v0

--- a/solution.py
+++ b/solution.py
@@ -2,6 +2,7 @@
 import jax.numpy as jnp
 from jax import lax
 from jax.sharding import PartitionSpec as P
+from jax.lax import all_to_all, axis_size
 
 NODES = 15
 BOTTOM = 8
@@ -95,7 +96,10 @@
     )
     second_off = off_one[None]
     second_diag = diag_one[None]
-    turned_one = lax.all_to_all(off_full, "row", split_axis=1, concat_axis=0, tiled=True)
+    turned_one = jnp.concatenate(
+        all_to_all(jnp.stack(jnp.split(off_full, axis_size("row"), axis=1), axis=0), "row", 0, 0),
+        axis=0,
+    )
     chain_two = jnp.stack(
         [jnp.concatenate([root_block, off_full], 1), jnp.concatenate([turned_one.T, diag_full], 1)],
         0,

time: 1250 us -> 1250 us (level)
  transfers between devices with their start and end apart: 15 -> 15, of which waited for: 13 -> 13; matrix products, arithmetic and copies ran while one was open for 23% -> 22% of each run, Pallas kernels for 0% -> 0%
where the time goes in v1:
time: 1250 us; the launch traced here: 1240 us
  waiting for transfers between devices  820 us (66%)
  local copies, waits for them, and re-layouts  226 us (18%)
  matrix products  83.2 us (7%)
  other arithmetic  71.5 us (6%)
  starting transfers between devices  22 us (2%)
  between operations  14.7 us (1%)
    all_to_all x1, waiting for transfers between devices, local(): lax.all_to_all(full_two, 'row', split_axis=2, concat_axis=1, tiled=True)  191 us
    reduce_scatter x1, waiting for transfers between devices, local(): lax.psum_scatter(term_three.astype(jnp.bfloat16), 'row', scatter_dimensio...  141 us
    gather x2, local copies, waits for them, and re-layouts, local(): jnp.take(flat_three, positions.reshape(-1), axis=1)  90.3 us
    all_gather x1, waiting for transfers between devices, local(): lax.all_gather(panel_two, 'row', axis=1, tiled=True)  82.6 us
    all_gather x1, waiting for transfers between devices, local(): full_three = lax.all_gather(off_three, 'col', axis=3, tiled=True)  79 us
    reduce_scatter x1, waiting for transfers between devices, local(): lax.psum_scatter(term_two.astype(jnp.bfloat16), 'row', scatter_dimension=...  74.7 us
    gather x3, local copies, waits for them, and re-layouts, local(): jnp.take(rows_in, picks, axis=0)  71.3 us
    all_to_all x1, waiting for transfers between devices, local(): all_to_all(jnp.stack(jnp.split(off_full, axis_size('row'), axis=1), axis=...  68.4 us
  transfers between devices with their start and end apart: 15, of which 13 were waited for; matrix products, arithmetic and copies ran while one was open for 22% of the time, Pallas kernels for 0%

profile of v1, /device:TPU:0, one launch (start us, length us, event | category | flops | bytes accessed | tf_op | source)
XLA Modules:
  0.0 1237.6 jit_solution(8056756718153811453)
XLA Ops:
  15.1 44.9 %all-gather.9.cloned.1.call-done = bf16[2048,512]{0,1:T(8,128)(2,1)} async-done(((bf16[512,512]{0,1:T(8,128)(2,1)}), bf16[2048,512]{0,1:T(8,128)(2,1)}) %all-gather.9.cloned.1.call-update) | async-done | bytes 2097168 | tf_op jit(solution)/shard_map/all_gather | solution.py:69
  63.7 20.2 %all-gather.11.cloned.1.call-done = bf16[512,1024]{1,0:T(8,128)(2,1)} async-done(((bf16[512,512]{1,0:T(8,128)(2,1)}), bf16[512,1024]{1,0:T(8,128)(2,1)}) %all-gather.11.cloned.1.call-update) | async-done | bytes 1048592 | tf_op jit(solution)/shard_map/all_gather | solution.py:73
  93.5 42.9 %reduce-scatter.4.cloned.1.call-done = bf16[512,512]{0,1:T(8,128)(2,1)} async-done(((bf16[512,2048]{0,1:T(8,128)(2,1)}), bf16[512,512]{0,1:T(8,128)(2,1)}) %reduce-scatter.4.cloned.1.call-update) | async-done | bytes 524304 | tf_op jit(solution)/shard_map/reduce_scatter | solution.py:83
  144.3 4.4 all-to-all-start
  148.8 10.6 all-gather.13.cloned.1.call-done
  163.3 68.4 %all-to-all-done = bf16[4,512,512]{2,1,0:T(8,128)(2,1)} async-done(((bf16[4,512,512]{2,1,0:T(8,128)(2,1)}), bf16[4,512,512]{2,1,0:T(8,128)(2,1)}, u32[]{:S(2)}, u32[]{:S(2)}) %all-to-all-start) | async-done | bytes 2097184 | tf_op jit(solution)/shard_map/all_to_all | solution.py:100
  242.1 7.6 pad_maximum_fusion.1
  249.7 82.6 %all-gather.15.cloned.1.call-done = bf16[2,2048,1024]{2,1,0:T(8,128)(2,1)} async-done(((bf16[2,512,1024]{2,1,0:T(8,128)(2,1)}), bf16[2,2048,1024]{2,1,0:T(8,128)(2,1)}) %all-gather.15.cloned.1.call-update) | async-done | bytes 8388624 | tf_op jit(solution)/shard_map/all_gather | solution.py:113
  332.3 14.6 %negate_convert_fusion = bf16[1024,1024]{1,0:T(8,128)(2,1)} fusion(bf16[1024,4096]{1,0:T(8,128)(2,1)} %bitcast.113, bf16[4096,1024]{1,0:T(8,128)(2,1)} %bitcast.122), kind=kOutput, calls=%fused_computation.21 | convolution fusion | flops 8592031744 | bytes 18874368 | tf_op jit(solution)/shard_map/dot_general | solution.py:35
  347.0 12.2 reduce-scatter.6.cloned.1.call-start
  359.2 43.7 %all-gather.17.cloned.1.call-done = bf16[2,512,2048]{2,1,0:T(8,128)(2,1)} async-done(((bf16[2,512,1024]{2,1,0:T(8,128)(2,1)}), bf16[2,512,2048]{2,1,0:T(8,128)(2,1)}) %all-gather.17.cloned.1.call-update) | async-done | bytes 4194320 | tf_op jit(solution)/shard_map/all_gather | solution.py:116
  402.9 9.4 bitcast_convert_fusion.1
  414.5 74.7 %reduce-scatter.6.cloned.1.call-done = bf16[1024,512]{0,1:T(8,128)(2,1)} async-done(((bf16[1024,2048]{0,1:T(8,128)(2,1)}), bf16[1024,512]{0,1:T(8,128)(2,1)}) %reduce-scatter.6.cloned.1.call-update) | async-done | bytes 1048592 | tf_op jit(solution)/shard_map/reduce_scatter | solution.py:118
  493.8 4.4 broadcast_select_fusion
  498.3 11.2 copy.62
  509.5 5.0 all-to-all-start.1
  520.9 5.1 maximum_bitcast_fusion
  526.0 191.2 %all-to-all-done.1 = bf16[2,512,2048]{1,0,2:T(2,128)(2,1)} async-done(((bf16[2,512,2048]{1,0,2:T(2,128)(2,1)}), bf16[2,512,2048]{1,0,2:T(2,128)(2,1)}, u32[]{:S(2)}, u32[]{:S(2)}) %all-to-all-start.1) | async-done | bytes 4194336 | tf_op jit(solution)/shard_map/all_to_all | solution.py:127
  717.2 5.1 copy.75
  722.2 4.5 copy.77
  726.7 6.4 maximum_bitcast_fusion.2
  733.1 12.1 pad_maximum_fusion
  745.2 24.7 %copy.64 = bf16[1536,6144]{0,1:T(8,128)(2,1)} copy(bf16[1536,6144]{1,0:T(8,128)(2,1)} %bitcast.105) | data formatting | bytes 37748736 | tf_op jit(solution)/shard_map/reshape | solution.py:137
  770.0 58.3 %gather_fusion = bf16[8192,1536]{1,0:T(8,128)(2,1)} fusion(bf16[1536,6144]{0,1:T(8,128)(2,1)} %copy.64, s32[8192]{0:T(1024)S(1)} %broadcast_clamp_fusion), kind=kCustom, calls=%fused_computation | custom fusion | bytes 50364416 | tf_op jit(solution)/shard_map/jit(_take)/gather | solution.py:162
  828.2 32.1 %copy.65 = bf16[1536,2,4096]{2,0,1:T(8,128)(2,1)} copy(bf16[1536,2,4096]{0,2,1:T(8,128)(2,1)} %bitcast.104) | data formatting | bytes 50331648 | tf_op jit(solution)/shard_map/jit(_take)/gather | solution.py:162
  860.3 18.1 %all-gather.21.cloned.1.call-done = bf16[2,4096,1024]{2,1,0:T(8,128)(2,1)} async-done(((bf16[2,1024,1024]{2,1,0:T(8,128)(2,1)}), bf16[2,4096,1024]{2,1,0:T(8,128)(2,1)}) %all-gather.21.cloned.1.call-update) | async-done | bytes 16777232 | tf_op jit(solution)/shard_map/all_gather | solution.py:159
  878.4 33.0 %select_convert_fusion = bf16[2,1536,1024]{2,1,0:T(8,128)(2,1)} fusion(bf16[2,4096,1024]{2,1,0:T(8,128)(2,1)} %all-gather.21.cloned.1.call-done, bf16[1536,2,4096]{2,0,1:T(8,128)(2,1)} %copy.65, pred[2,4096]{1,0:T(4,128)(4,1)S(1)} %compare_and_fusion, pred[2,1536]{1,0:T(4,128)(4,1)S(1)} %compare_reduce_fusion), kind=kOutput, calls=%fused_computation.7 | convolution fusion | flops 25791823872 | bytes 48245760 | tf_op jit(solution)/shard_map/aec,ecn->ean/dot_general | solution.py:165
  912.4 62.6 %gather_fusion.1 = bf16[3072,1024]{1,0:T(8,128)(2,1)} fusion(bf16[2,4096,1024]{2,1,0:T(8,128)(2,1)} %all-gather.21.cloned.1.call-done, s32[3072]{0:T(1024)S(1)} %reshape.370), kind=kCustom, calls=%fused_computation.1 | custom fusion | bytes 12607488 | tf_op jit(solution)/shard_map/vmap(jit(_take))/gather | solution.py:167
  975.1 8.7 copy.66
  983.7 79.0 %all-gather.23.cloned.1.call-done = bf16[2,3,512,2048]{3,2,1,0:T(8,128)(2,1)} async-done(((bf16[2,3,512,1024]{3,2,1,0:T(8,128)(2,1)}), bf16[2,3,512,2048]{3,2,1,0:T(8,128)(2,1)}) %all-gather.23.cloned.1.call-update) | async-done | bytes 12582928 | tf_op jit(solution)/shard_map/all_gather | solution.py:175
  1062.7 20.0 %bitcast_convert_fusion = bf16[2,1024,2048]{2,1,0:T(8,128)(2,1)} fusion(bf16[2,3,512,2048]{3,2,1,0:T(8,128)(2,1)} %all-gather.23.cloned.1.call-done, bf16[2,3,512,1024]{2,3,1,0:T(8,128)(2,1)} %copy.66, pred[2,3,512]{2,1,0:T(4,128)(4,1)S(1)} %get-tuple-element.44, pred[2,3,512]{2,1,0:T(4,128)(4,1)S(1)} %get-tuple-element.43), kind=kOutput, calls=%fused_computation.6 | convolution fusion | flops 12895387648 | bytes 27269120 | tf_op jit(solution)/shard_map/ekin,ekim->enm/dot_general | solution.py:176
  1087.0 140.5 %reduce-scatter.8.cloned.1.call-done = bf16[2,1024,512]{2,1,0:T(8,128)(2,1)} async-done(((bf16[2,1024,2048]{2,1,0:T(8,128)(2,1)}), bf16[2,1024,512]{2,1,0:T(8,128)(2,1)}) %reduce-scatter.8.cloned.1.call-update) | async-done | bytes 2097168 | tf_op jit(solution)/shard_map/reduce_scatter | solution.py:179
  (134 shorter events, 64.8 us)
Async XLA Ops:
  7.2 52.8 %all-gather.9.cloned.1.call-start = ((), (), s32[]{:S(2)}) async-start(), calls=%async_computation.5 | async-start | bytes 2621440 | tf_op jit(solution)/shard_map/all_gather | solution.py:69
  11.4 72.5 %all-gather.11.cloned.1.call-start = ((), (), s32[]{:S(2)}) async-start(), calls=%async_computation.6 | async-start | bytes 1572864 | tf_op jit(solution)/shard_map/all_gather | solution.py:73
  15.1 48.6 %copy-start = (bf16[512,2048]{1,0:T(8,128)(2,1)}, bf16[512,2048]{1,0:T(8,128)(2,1)S(1)}, u32[]{:S(2)}) copy-start(bf16[512,2048]{1,0:T(8,128)(2,1)S(1)} %and_select_fusion.1) | copy-start | bytes 6291460
  63.7 26.3 %copy-start.8 = (bf16[512,512]{0,1:T(8,128)(2,1)S(1)}, bf16[512,512]{0,1:T(8,128)(2,1)}, u32[]{:S(2)}) copy-start(bf16[512,512]{0,1:T(8,128)(2,1)} %bitcast_select_fusion.1) | copy-start | bytes 1572868
  63.7 72.7 %reduce-scatter.4.cloned.1.call-start = ((), (), s32[]{:S(2)}) async-start(), calls=%async_computation.7 | async-start | bytes 2621440 | tf_op jit(solution)/shard_map/reduce_scatter | solution.py:83
  83.9 3.0 collective-permute-start
  89.9 2.7 copy-start.10
  92.6 66.8 %all-gather.13.cloned.1.call-start = ((), (), s32[]{:S(2)}) async-start(), calls=%async_computation.8 | async-start | bytes 1572864 | tf_op jit(solution)/shard_map/all_gather | solution.py:90
  138.7 193.6 %all-gather.15.cloned.1.call-start = ((), (), s32[]{:S(2)}) async-start(), calls=%async_computation.9 | async-start | bytes 10485760 | tf_op jit(solution)/shard_map/all_gather | solution.py:113
  144.3 87.4 %all-to-all-start = ((bf16[4,512,512]{2,1,0:T(8,128)(2,1)}), bf16[4,512,512]{2,1,0:T(8,128)(2,1)}, u32[]{:S(2)}, u32[]{:S(2)}) async-start(bf16[4,512,512]{2,1,0:T(8,128)(2,1)} %pad_maximum_fusion.2), calls=%async_computation.1 | async-start | bytes 4194304 | tf_op jit(solution)/shard_map/all_to_all | solution.py:100
  148.8 254.1 %all-gather.17.cloned.1.call-start = ((), (), s32[]{:S(2)}) async-start(), calls=%async_computation.10 | async-start | bytes 6291456 | tf_op jit(solution)/shard_map/all_gather | solution.py:116
  159.4 76.3 %collective-permute-start.1 = (bf16[512,1024]{1,0:T(8,128)(2,1)}, bf16[512,1024]{1,0:T(8,128)(2,1)}, u32[]{:S(2)}, u32[]{:S(2)}) collective-permute-start(bf16[512,1024]{1,0:T(8,128)(2,1)} %all-gather.13.cloned.1.call-done), channel_id=1, source_target_pairs={{0,8},{8,0},{16,24},{24,16},{1,9},{9,1},{17,25},{25,17},{2,10},{10... | collective-permute-start | bytes 3145736 | tf_op jit(solution)/shard_map/ppermute | solution.py:18
  163.3 72.4 %copy-start.9 = (bf16[512,1024]{1,0:T(8,128)(2,1)S(1)}, bf16[512,1024]{1,0:T(8,128)(2,1)}, u32[]{:S(2)}) copy-start(bf16[512,1024]{1,0:T(8,128)(2,1)} %all-gather.13.cloned.1.call-done) | copy-start | bytes 3145732
  235.7 3.9 copy-start.2
  238.2 1.4 copy-start.4
  347.0 142.3 %reduce-scatter.6.cloned.1.call-start = ((), (), s32[]{:S(2)}) async-start(), calls=%async_computation.11 | async-start | bytes 5242880 | tf_op jit(solution)/shard_map/reduce_scatter | solution.py:118
  412.3 80.1 %copy-start.23 = (s32[15]{0:T(128)S(1)}, s32[15]{0:T(128)}, u32[]{:S(2)}) copy-start(s32[15]{0:T(128)} %param.9) | copy-start | bytes 184
  412.3 314.4 %all-gather.19.cloned.1.call-start = ((), (), s32[]{:S(2)}) async-start(), calls=%async_computation.12 | async-start | bytes 3145728 | tf_op jit(solution)/shard_map/all_gather | solution.py:126
  492.3 386.1 %all-gather.21.cloned.1.call-start = ((), (), s32[]{:S(2)}) async-start(), calls=%async_computation.13 | async-start | bytes 20971520 | tf_op jit(solution)/shard_map/all_gather | solution.py:159
  509.5 6.4 copy-start.19
  509.5 207.6 %all-to-all-start.1 = ((bf16[2,512,2048]{1,0,2:T(2,128)(2,1)}), bf16[2,512,2048]{1,0,2:T(2,128)(2,1)}, u32[]{:S(2)}, u32[]{:S(2)}) async-start(bf16[2,512,2048]{1,0,2:T(2,128)(2,1)} %copy.62), calls=%async_computation.3 | async-start | bytes 8388608 | tf_op jit(solution)/shard_map/all_to_all | solution.py:127
  514.5 548.2 %all-gather.23.cloned.1.call-start = ((), (), s32[]{:S(2)}) async-start(), calls=%async_computation.14 | async-start | bytes 18874368 | tf_op jit(solution)/shard_map/all_gather | solution.py:175
  516.7 2.9 copy-start.1
  516.8 3.5 copy-start.3
  516.8 4.1 copy-start.5
  726.7 6.4 slice-start
  726.7 6.4 slice-start.1
  911.4 0.9 copy-start.15
  911.5 316.0 %reduce-scatter.8.cloned.1.call-start = ((), (), s32[]{:S(2)}) async-start(), calls=%async_computation.15 | async-start | bytes 10485760 | tf_op jit(solution)/shard_map/reduce_scatter | solution.py:179
  1082.7 3.0 copy-start.6
  1082.7 144.8 %copy-start.7 = (bf16[2,1024,512]{2,1,0:T(8,128)(2,1)S(1)}, bf16[2,1024,512]{2,1,0:T(8,128)(2,1)}, u32[]{:S(2)}) copy-start(bf16[2,1024,512]{2,1,0:T(8,128)(2,1)} %param.17) | copy-start | bytes 6291460
  1082.7 144.8 %copy-start.14 = (pred[2,1024]{1,0:T(4,128)(4,1)S(1)}, pred[2,1024]{1,0:T(4,128)(4,1)}, u32[]{:S(2)}) copy-start(pred[2,1024]{1,0:T(4,128)(4,1)} %copy-done.13) | copy-start | bytes 6148
  (9 other events, 6.0 us)
Sparse Core Ops, SparseCore 0:
  11.6 48.3 all-gather.8
  63.8 20.0 all-gather.10
  92.7 43.6 reduce-scatter.3
  138.9 20.4 all-gather.12
  160.8 171.4 all-gather.14
  347.1 55.7 all-gather.16
  412.4 76.7 reduce-scatter.5
  492.5 33.6 all-gather.18
  527.7 350.6 all-gather.20
  911.6 151.0 all-gather.22
  1082.8 144.6 reduce-scatter.7
